TPU v7x, 32 devices: a whole 2x2x4 slice. The times are simulated.
32 devices in a mesh: dp: 2 (over x), expert: 16 (over z, y, core).
Axes of the slice: x: 2, y: 2, z: 4, core: 2. Of those that a mesh axis runs over, the one named last changes fastest.
Arguments:
- tokens: bfloat16 [2048, 2048], P('expert'), may hold values from -6 to 6
- routing: int32 [2048, 8], P('expert'), may hold values from 0 to 31, all different within a row; in each aligned block of 128 rows (0 to 127, 128 to 255, ...) at most 48 rows name the same one
- route_gates: float32 [2048, 8], P('expert'), may hold values from 0.03 to 0.3
- gate_weight: bfloat16 [32, 2048, 768], P('expert', None, 'dp'), may hold values from -0.125 to 0.125
- up_weight: bfloat16 [32, 2048, 768], P('expert', None, 'dp'), may hold values from -0.125 to 0.125
- down_weight: bfloat16 [32, 2048, 768], P('expert', None, 'dp'), may hold values from -0.21875 to 0.21875
- cotangent: bfloat16 [2048, 2048], P('expert'), may hold values from -4 to 4
Outputs:
- mixed: bfloat16 [2048, 2048], P('expert', 'dp')
- token_grad: bfloat16 [2048, 2048], P('expert', 'dp')
- gates_grad: float32 [2048, 8], P('expert')
- gate_grad: bfloat16 [32, 2048, 768], P('expert', None, 'dp')
- up_grad: bfloat16 [32, 2048, 768], P('expert', None, 'dp')
- down_grad: bfloat16 [32, 2048, 768], P('expert', None, 'dp')
Inputs may be any that keep to these rules, and one draw needn't show every extreme that they name: `routing`: each row names 8 different experts. Among the rows of one index of expert (aligned blocks of 128 rows) no expert is named more than 48 times, a bound that some block reaches.
All inputs are finite; a program needn't handle non-finite values.
Results may differ from a plain program's by a relative error of at most 0.012.
Values may be sent and summed in bfloat16 or wider, within the bound.
A program may use at most 192 MiB of HBM per device.

v0:
```python
import jax
import jax.numpy as jnp
from jax import lax
from jax.sharding import PartitionSpec as P


def expert_forward(slot_rows, w_gate, w_up, w_down):
    gate_pre = jnp.einsum("jrd,jdf->jrf", slot_rows, w_gate, preferred_element_type=jnp.float32)
    up_pre = jnp.einsum("jrd,jdf->jrf", slot_rows, w_up, preferred_element_type=jnp.float32)
    sigmoid_gate = jax.nn.sigmoid(gate_pre)
    active = gate_pre * sigmoid_gate
    hidden = (active * up_pre).astype(jnp.bfloat16)
    out_part = jnp.einsum("jrf,jdf->jrd", hidden, w_down, preferred_element_type=jnp.float32)
    return (out_part, (gate_pre, up_pre, sigmoid_gate, active, hidden))


def expert_backward(slot_rows, slot_back, saved, w_gate, w_up, w_down):
    gate_pre, up_pre, sigmoid_gate, active, hidden = saved
    dhidden = jnp.einsum("jrd,jdf->jrf", slot_back, w_down, preferred_element_type=jnp.float32)
    d_gate = (dhidden * up_pre * sigmoid_gate * (1.0 + gate_pre * (1.0 - sigmoid_gate))).astype(
        jnp.bfloat16
    )
    d_up = (dhidden * active).astype(jnp.bfloat16)
    row_part = jnp.einsum("jrf,jdf->jrd", d_gate, w_gate, preferred_element_type=jnp.float32)
    row_part = row_part + jnp.einsum("jrf,jdf->jrd", d_up, w_up, preferred_element_type=jnp.float32)
    grad_g = jnp.einsum("jrd,jrf->jdf", slot_rows, d_gate, preferred_element_type=jnp.float32)
    grad_u = jnp.einsum("jrd,jrf->jdf", slot_rows, d_up, preferred_element_type=jnp.float32)
    grad_d = jnp.einsum("jrd,jrf->jdf", slot_back, hidden, preferred_element_type=jnp.float32)
    return (row_part, (grad_g, grad_u, grad_d))


def body(tokens, routing, route_gates, gate_weight, up_weight, down_weight, cotangent):
    rows_here, width = tokens.shape
    picks = routing.shape[1]
    local_count = gate_weight.shape[0]
    devices = lax.axis_size("expert")
    experts_all = local_count * devices
    capacity = 3 * rows_here * picks // (2 * experts_all)
    member = lax.axis_index("dp")
    chosen = routing.reshape(-1)
    one_hot = (chosen[:, None] == jnp.arange(experts_all, dtype=jnp.int32)[None, :]).astype(
        jnp.int32
    )
    running = jnp.cumsum(one_hot, axis=0) - one_hot
    within = jnp.sum(running * one_hot, axis=1)
    owners = chosen // local_count
    slots = chosen % local_count
    source_row = jnp.arange(rows_here * picks, dtype=jnp.int32) // picks
    flat_gates = route_gates.reshape(-1)
    x_rows = tokens[source_row]
    weighted = (flat_gates[:, None] * cotangent[source_row].astype(jnp.float32)).astype(
        jnp.bfloat16
    )
    half_cap = (capacity + 1) // 2
    mine = within // half_cap == member
    local_within = jnp.clip(within - member * half_cap, 0, half_cap - 1)
    target = jnp.where(mine, owners, devices)

    def scatter_share(values):
        buffer = jnp.zeros((local_count, devices, half_cap) + values.shape[1:], values.dtype)
        return buffer.at[slots, target, local_within].set(values, mode="drop")

    def gather_share(buffer):
        picked = buffer.at[slots, target, local_within].get(mode="fill", fill_value=0)
        return jnp.where(mine[:, None], picked, jnp.zeros((), picked.dtype))

    full_gate, full_up, full_down = (
        lax.all_gather(gate_weight, "dp", axis=2, tiled=True),
        lax.all_gather(up_weight, "dp", axis=2, tiled=True),
        lax.all_gather(down_weight, "dp", axis=2, tiled=True),
    )
    got_rows, got_back = (
        lax.all_to_all(scatter_share(x_rows), "expert", split_axis=1, concat_axis=1, tiled=True),
        lax.all_to_all(scatter_share(weighted), "expert", split_axis=1, concat_axis=1, tiled=True),
    )
    slot_rows = got_rows.reshape(local_count, devices * half_cap, width)
    slot_back = got_back.reshape(local_count, devices * half_cap, width)
    out_full, saved = expert_forward(slot_rows, full_gate, full_up, full_down)
    row_full, grads_full = expert_backward(
        slot_rows, slot_back, saved, full_gate, full_up, full_down
    )
    share_shape = (local_count, devices, half_cap, width)
    back_out, back_grad = (
        lax.all_to_all(
            out_full.astype(jnp.bfloat16).reshape(share_shape),
            "expert",
            split_axis=1,
            concat_axis=1,
            tiled=True,
        ),
        lax.all_to_all(
            row_full.astype(jnp.bfloat16).reshape(share_shape),
            "expert",
            split_axis=1,
            concat_axis=1,
            tiled=True,
        ),
    )
    expert_rows = gather_share(back_out).reshape(rows_here, picks, width)
    grad_rows = gather_share(back_grad).reshape(rows_here, picks, width)
    gate_part = jnp.einsum("td,tkd->tk", cotangent, expert_rows, preferred_element_type=jnp.float32)
    mixed_part = jnp.einsum("tk,tkd->td", route_gates, expert_rows.astype(jnp.float32))
    token_part = jnp.sum(grad_rows.astype(jnp.float32), axis=1)
    mixed_sum, token_sum = (
        lax.psum_scatter(
            mixed_part.astype(jnp.bfloat16), "dp", scatter_dimension=1, tiled=True
        ).astype(jnp.float32),
        lax.psum_scatter(
            token_part.astype(jnp.bfloat16), "dp", scatter_dimension=1, tiled=True
        ).astype(jnp.float32),
    )
    mixed = mixed_sum.astype(jnp.bfloat16)
    token_grad = token_sum.astype(jnp.bfloat16)
    grad_g, grad_u, grad_d = (
        lax.psum_scatter(
            grads_full[0].astype(jnp.bfloat16), "dp", scatter_dimension=2, tiled=True
        ).astype(jnp.float32),
        lax.psum_scatter(
            grads_full[1].astype(jnp.bfloat16), "dp", scatter_dimension=2, tiled=True
        ).astype(jnp.float32),
        lax.psum_scatter(
            grads_full[2].astype(jnp.bfloat16), "dp", scatter_dimension=2, tiled=True
        ).astype(jnp.float32),
    )
    grad_g = grad_g.astype(jnp.bfloat16)
    grad_u = grad_u.astype(jnp.bfloat16)
    grad_d = grad_d.astype(jnp.bfloat16)
    gates_grad = lax.psum(gate_part, "dp")
    return (mixed, token_grad, gates_grad, grad_g, grad_u, grad_d)


def solution(mesh):
    in_specs = (
        P("expert", None),
        P("expert", None),
        P("expert", None),
        P("expert", None, "dp"),
        P("expert", None, "dp"),
        P("expert", None, "dp"),
        P("expert", None),
    )
    out_specs = (
        P("expert", "dp"),
        P("expert", "dp"),
        P("expert", None),
        P("expert", None, "dp"),
        P("expert", None, "dp"),
        P("expert", None, "dp"),
    )
    return jax.shard_map(body, mesh=mesh, in_specs=in_specs, out_specs=out_specs, check_vma=False)
```

profile of v0, /device:TPU:16, one launch (start us, length us, event | category | flops | bytes accessed | tf_op | source)
XLA Modules:
  0.0 631.3 jit_solution(1419961133742807753)
XLA Ops:
  7.3 0.7 all-gather.4.cloned.1.call-update
  8.0 0.1 copy.40
  8.1 0.1 eq.51
  8.2 0.1 eq.47
  8.3 0.1 reshape.312
  8.4 9.0 %reduce-window.6 = s32[32,8,128]{2,1,0:T(8,128)S(1)} reduce-window(s32[32,8,128]{2,1,0:T(8,128)S(1)} %fusion.20, s32[]{:T(128)} %constant.64.clone.1), window={size=1x1x128 pad=0_0x0_0x127_0}, to_apply=%region_0.0 | reduce-window | flops 4161536 | bytes 262148 | tf_op jit(solution)/shard_map/reduce-window
  17.5 0.1 copy.42
  17.8 0.1 broadcast_add_fusion
  18.1 0.1 and_reduce_fusion.1
  18.3 22.2 %scatter_custom_fusion = bf16[768,2048]{1,0:T(8,128)(2,1)} fusion(s32[1024]{0:T(1024)S(1)} %get-tuple-element.18, bf16[128,2048]{1,0:T(8,128)(2,1)} %param.7, s32[1024]{0:T(1024)S(1)} %get-tuple-element.17, bf16[]{:T(256)} %constant.75.clone.1), kind=kCustom, calls=%fused_computation.17 | custom fusion | bytes 3146240
  40.4 4.0 copy.45
  44.4 6.3 %all-to-all-start = ((bf16[2,16,24,2048]{3,2,0,1:T(8,128)(2,1)}), bf16[2,16,24,2048]{3,2,0,1:T(8,128)(2,1)}, u32[]{:S(2)}, u32[]{:S(2)}) async-start(bf16[2,16,24,2048]{3,2,0,1:T(8,128)(2,1)} %copy.45), calls=%async_computation | async-start | bytes 6291456 | tf_op jit(solution)/shard_map/all_to_all | solution.py:73
  50.7 0.5 all-gather.6.cloned.1.call-start
  51.2 0.2 all-gather.6.cloned.1.call-update
  51.5 0.1 copy.49
  51.6 0.1 mul.41
  51.7 22.4 %scatter_custom_fusion.1 = bf16[768,2048]{1,0:T(8,128)(2,1)} fusion(s32[1024]{0:T(1024)S(1)} %get-tuple-element.18, f32[1024]{0:T(1024)S(1)} %mul.41, bf16[]{:T(256)} %constant.75.clone.1, bf16[128,2048]{1,0:T(8,128)(2,1)S(1)} %copy-done, s32[1024]{0:T(1024)S(1)} %get-tuple-element.17), kind=kCustom, calls=%fused_computation.11 | custom fusion | flops 6291456 | bytes 3678210
  74.1 4.0 copy.50
  78.1 42.8 %all-to-all-done = bf16[2,16,24,2048]{3,2,0,1:T(8,128)(2,1)} async-done(((bf16[2,16,24,2048]{3,2,0,1:T(8,128)(2,1)}), bf16[2,16,24,2048]{3,2,0,1:T(8,128)(2,1)}, u32[]{:S(2)}, u32[]{:S(2)}) %all-to-all-start) | async-done | bytes 3145760 | tf_op jit(solution)/shard_map/all_to_all | solution.py:73
  120.9 4.6 all-to-all-start.2
  125.5 0.7 all-gather.8.cloned.1.call-update
  126.3 4.0 copy.46
  130.3 65.4 %all-to-all-done.2 = bf16[2,16,24,2048]{3,2,0,1:T(8,128)(2,1)} async-done(((bf16[2,16,24,2048]{3,2,0,1:T(8,128)(2,1)}), bf16[2,16,24,2048]{3,2,0,1:T(8,128)(2,1)}, u32[]{:S(2)}, u32[]{:S(2)}) %all-to-all-start.2) | async-done | bytes 3145760 | tf_op jit(solution)/shard_map/all_to_all | solution.py:74
  195.7 4.0 copy.51
  199.7 7.7 %fusion.26 = f32[2,384,768]{2,1,0:T(8,128)} fusion(bf16[2,384,2048]{2,1,0:T(8,128)(2,1)} %bitcast.93, bf16[2,2048,768]{2,1,0:T(8,128)(2,1)} %all-gather.4.cloned.1.call-done), kind=kOutput, calls=%fused_computation.74 | convolution fusion | flops 2415919104 | bytes 11796480 | tf_op jit(solution)/shard_map/jrd,jdf->jrf/dot_general | solution.py:8
  207.4 7.8 %fusion.27 = f32[2,384,768]{2,1,0:T(8,128)} fusion(bf16[2,384,2048]{2,1,0:T(8,128)(2,1)} %bitcast.94, bf16[2,2048,768]{2,1,0:T(8,128)(2,1)} %all-gather.6.cloned.1.call-done), kind=kOutput, calls=%fused_computation.75 | convolution fusion | flops 2415919104 | bytes 11796480 | tf_op jit(solution)/shard_map/jrd,jdf->jrf/dot_general | solution.py:9
  215.2 39.7 %all-gather.8.cloned.1.call-done = bf16[2,2048,768]{2,1,0:T(8,128)(2,1)} async-done(((bf16[2,2048,384]{2,1,0:T(8,128)(2,1)}), bf16[2,2048,768]{2,1,0:T(8,128)(2,1)}) %all-gather.8.cloned.1.call-update) | async-done | bytes 6291472 | tf_op jit(solution)/shard_map/all_gather | solution.py:70
  254.9 9.5 %multiply_convert_fusion.2 = (bf16[2,384,768]{2,1,0:T(8,128)(2,1)S(1)}, bf16[2,384,768]{2,1,0:T(8,128)(2,1)S(1)}, bf16[2,384,768]{2,1,0:T(8,128)(2,1)}) fusion(f32[2,384,768]{2,1,0:T(8,128)} %fusion.26, f32[2,384,768]{2,1,0:T(8,128)} %fusion.27, bf16[2,384,2048]{2,1,0:T(8,128)(2,1)} %bitcast.91, bf16[2,2048,768]{2,1,0:T(8,128)(2,1)} %all-gather.8.cloned.1.call-done), kind=kOutput, calls=%fused_computation.23 | convolution fusion | flops 2424766464 | bytes 17694720 | tf_op jit(solution)/shard_map/jrd,jdf->jrf/dot_general | solution.py:19
  264.4 5.6 convolution_convert_fusion.2
  269.9 16.4 %copy.64 = bf16[2,2048,768]{1,0,2:T(2,128)(2,1)} copy(bf16[2,2048,768]{2,1,0:T(8,128)(2,1)} %convolution_convert_fusion.2) | data formatting | bytes 12582912
  286.3 9.4 %copy.71 = bf16[96,8,2,2048]{3,1,2,0:T(8,128)(2,1)} copy(bf16[96,8,2,2048]{3,2,1,0:T(2,128)(2,1)} %bitcast.83) | data formatting | bytes 12582912
  295.8 8.5 %convolution_convert_fusion.1 = bf16[2,2048,768]{2,1,0:T(8,128)(2,1)} fusion(bf16[2,384,2048]{2,1,0:T(8,128)(2,1)} %bitcast.95, bf16[2,384,768]{2,1,0:T(8,128)(2,1)S(1)} %get-tuple-element.11), kind=kOutput, calls=%fused_computation.9 | convolution fusion | flops 2419064832 | bytes 10616832 | tf_op jit(solution)/shard_map/jrd,jrf->jdf/dot_general | solution.py:27
  304.3 16.7 %copy.66 = bf16[2,2048,768]{1,0,2:T(2,128)(2,1)} copy(bf16[2,2048,768]{2,1,0:T(8,128)(2,1)} %convolution_convert_fusion.1) | data formatting | bytes 12582912
  321.0 9.7 %copy.72 = bf16[96,8,2,2048]{3,1,2,0:T(8,128)(2,1)} copy(bf16[96,8,2,2048]{3,2,1,0:T(2,128)(2,1)} %bitcast.84) | data formatting | bytes 12582912
  330.9 8.6 %convolution_convert_fusion = bf16[2,2048,768]{2,1,0:T(8,128)(2,1)} fusion(bf16[2,384,2048]{2,1,0:T(8,128)(2,1)} %bitcast.92, bf16[2,384,768]{2,1,0:T(8,128)(2,1)} %get-tuple-element.13), kind=kOutput, calls=%fused_computation.8 | convolution fusion | flops 2419064832 | bytes 10616832 | tf_op jit(solution)/shard_map/jrd,jrf->jdf/dot_general | solution.py:28
  339.4 16.8 %copy.68 = bf16[2,2048,768]{1,0,2:T(2,128)(2,1)} copy(bf16[2,2048,768]{2,1,0:T(8,128)(2,1)} %convolution_convert_fusion) | data formatting | bytes 12582912
  356.3 9.5 %copy.73 = bf16[96,8,2,2048]{3,1,2,0:T(8,128)(2,1)} copy(bf16[96,8,2,2048]{3,2,1,0:T(2,128)(2,1)} %bitcast.85) | data formatting | bytes 12582912
  365.8 5.8 convolution_convert_fusion.3
  371.6 1.9 copy.47
  373.5 6.0 all-to-all-start.1
  379.5 5.1 fusion.28
  384.7 7.2 %add_convert_fusion = bf16[2,384,2048]{2,1,0:T(8,128)(2,1)S(1)} fusion(f32[2,384,2048]{2,1,0:T(8,128)S(1)} %fusion.28, bf16[2,384,768]{2,1,0:T(8,128)(2,1)S(1)} %get-tuple-element.11, bf16[2,2048,768]{2,1,0:T(8,128)(2,1)} %all-gather.6.cloned.1.call-done), kind=kOutput, calls=%fused_computation.7 | convolution fusion | flops 2419064832 | bytes 16908288 | tf_op jit(solution)/shard_map/jrf,jdf->jrd/dot_general | solution.py:25
  391.9 1.9 copy.52
  393.8 56.0 %all-to-all-done.1 = bf16[2,16,24,2048]{3,2,0,1:T(8,128)(2,1)} async-done(((bf16[2,16,24,2048]{3,2,0,1:T(8,128)(2,1)}), bf16[2,16,24,2048]{3,2,0,1:T(8,128)(2,1)}, u32[]{:S(2)}, u32[]{:S(2)}) %all-to-all-start.1) | async-done | bytes 3145760 | tf_op jit(solution)/shard_map/all_to_all | solution.py:84
  449.7 4.6 all-to-all-start.3
  454.3 0.1 and.80
  454.5 0.1 copy.57
  454.7 0.1 broadcast_in_dim.24
  454.8 4.0 copy.48
  458.8 35.8 %gather_fusion = bf16[1024,2048]{1,0:T(8,128)(2,1)} fusion(bf16[2,16,24,2048]{3,2,1,0:T(8,128)(2,1)} %copy.48, s32[1024]{0:T(1024)S(1)} %bitcast.78), kind=kCustom, calls=%fused_computation.1 | custom fusion | bytes 8400896 | tf_op jit(solution)/shard_map/gather | solution.py:64
  494.6 3.6 fusion.9
  498.1 1.1 copy.78
  499.3 25.2 %all-to-all-done.3 = bf16[2,16,24,2048]{3,2,0,1:T(8,128)(2,1)} async-done(((bf16[2,16,24,2048]{3,2,0,1:T(8,128)(2,1)}), bf16[2,16,24,2048]{3,2,0,1:T(8,128)(2,1)}, u32[]{:S(2)}, u32[]{:S(2)}) %all-to-all-start.3) | async-done | bytes 3145760 | tf_op jit(solution)/shard_map/all_to_all | solution.py:91
  524.5 4.0 copy.53
  528.5 35.3 %gather_fusion.1 = bf16[1024,2048]{1,0:T(8,128)(2,1)} fusion(bf16[2,16,24,2048]{3,2,1,0:T(8,128)(2,1)} %copy.53, s32[1024]{0:T(1024)S(1)} %bitcast.79), kind=kCustom, calls=%fused_computation.3 | custom fusion | bytes 8400896 | tf_op jit(solution)/shard_map/gather | solution.py:64
  563.7 4.9 fusion.2
  568.7 5.4 fusion.7
  574.2 5.7 psum.7
  579.9 6.1 reshape.370
  586.0 8.7 %copy.65 = bf16[2,2048,384]{2,1,0:T(8,128)(2,1)} copy(bf16[2,2048,384]{1,0,2:T(2,128)(2,1)} %bitcast.86) | data formatting | bytes 6291456
  594.7 6.1 reshape.372
  600.8 8.7 %copy.67 = bf16[2,2048,384]{2,1,0:T(8,128)(2,1)} copy(bf16[2,2048,384]{1,0,2:T(2,128)(2,1)} %bitcast.87) | data formatting | bytes 6291456
  609.5 6.1 reshape.374
  615.6 8.7 %copy.69 = bf16[2,2048,384]{2,1,0:T(8,128)(2,1)} copy(bf16[2,2048,384]{1,0,2:T(2,128)(2,1)} %bitcast.88) | data formatting | bytes 6291456
  (48 shorter events, 1.0 us)
Async XLA Ops:
  7.2 44.5 %copy-start = (bf16[128,2048]{1,0:T(8,128)(2,1)S(1)}, bf16[128,2048]{1,0:T(8,128)(2,1)}, u32[]{:S(2)}) copy-start(bf16[128,2048]{1,0:T(8,128)(2,1)} %param.13) | copy-start | bytes 1572868
  7.2 10.8 %copy-start.6 = (s32[3]{0:T(128)S(1)}, s32[3]{0:T(128)}, u32[]{:S(2)}) copy-start(s32[3]{0:T(128)} %constant.83) | copy-start | bytes 40
  7.2 10.9 %copy-start.4 = (s32[3]{0:T(128)S(1)}, s32[3]{0:T(128)}, u32[]{:S(2)}) copy-start(s32[3]{0:T(128)} %constant.73.clone.1) | copy-start | bytes 40
  7.2 10.9 %copy-start.5 = (s32[3]{0:T(128)S(1)}, s32[3]{0:T(128)}, u32[]{:S(2)}) copy-start(s32[3]{0:T(128)} %constant.86) | copy-start | bytes 40
  7.2 0.7 copy-start.3
  7.2 192.4 %all-gather.4.cloned.1.call-start = ((), (), s32[]{:S(2)}) async-start(), calls=%async_computation.9 | async-start | bytes 9437184 | tf_op jit(solution)/shard_map/all_gather | solution.py:68
  44.4 7.1 %copy-start.2 = (f32[128,8]{0,1:T(8,128)S(1)}, f32[128,8]{0,1:T(8,128)}, u32[]{:S(2)}) copy-start(f32[128,8]{0,1:T(8,128)} %param.9) | copy-start | bytes 12292
  44.4 76.5 %all-to-all-start = ((bf16[2,16,24,2048]{3,2,0,1:T(8,128)(2,1)}), bf16[2,16,24,2048]{3,2,0,1:T(8,128)(2,1)}, u32[]{:S(2)}, u32[]{:S(2)}) async-start(bf16[2,16,24,2048]{3,2,0,1:T(8,128)(2,1)} %copy.45), calls=%async_computation | async-start | bytes 6291456 | tf_op jit(solution)/shard_map/all_to_all | solution.py:73
  50.7 156.7 %all-gather.6.cloned.1.call-start = ((), (), s32[]{:S(2)}) async-start(), calls=%async_computation.10 | async-start | bytes 9437184 | tf_op jit(solution)/shard_map/all_gather | solution.py:69
  120.9 74.8 %all-to-all-start.2 = ((bf16[2,16,24,2048]{3,2,0,1:T(8,128)(2,1)}), bf16[2,16,24,2048]{3,2,0,1:T(8,128)(2,1)}, u32[]{:S(2)}, u32[]{:S(2)}) async-start(bf16[2,16,24,2048]{3,2,0,1:T(8,128)(2,1)} %copy.50), calls=%async_computation.3 | async-start | bytes 6291456 | tf_op jit(solution)/shard_map/all_to_all | solution.py:74
  125.5 129.4 %all-gather.8.cloned.1.call-start = ((), (), s32[]{:S(2)}) async-start(), calls=%async_computation.11 | async-start | bytes 9437184 | tf_op jit(solution)/shard_map/all_gather | solution.py:70
  126.2 453.7 %reduce-scatter.16.cloned.1.call-start = ((), (), s32[]{:S(2)}) async-start(), calls=%async_computation.14 | async-start | bytes 9437184
  254.9 9.5 %copy-start.1 = (bf16[2,16,24,2048]{3,2,1,0:T(8,128)(2,1)S(1)}, bf16[2,16,24,2048]{3,2,1,0:T(8,128)(2,1)}, u32[]{:S(2)}) copy-start(bf16[2,16,24,2048]{3,2,1,0:T(8,128)(2,1)} %copy.46) | copy-start | bytes 9437188
  295.8 298.9 %reduce-scatter.18.cloned.1.call-start = ((), (), s32[]{:S(2)}) async-start(), calls=%async_computation.15 | async-start | bytes 9437184
  330.8 278.7 %reduce-scatter.20.cloned.1.call-start = ((), (), s32[]{:S(2)}) async-start(), calls=%async_computation.16 | async-start | bytes 9437184
  373.5 76.2 %all-to-all-start.1 = ((bf16[2,16,24,2048]{3,2,0,1:T(8,128)(2,1)}), bf16[2,16,24,2048]{3,2,0,1:T(8,128)(2,1)}, u32[]{:S(2)}, u32[]{:S(2)}) async-start(bf16[2,16,24,2048]{3,2,0,1:T(8,128)(2,1)} %copy.47), calls=%async_computation.1 | async-start | bytes 6291456 | tf_op jit(solution)/shard_map/all_to_all | solution.py:84
  449.7 74.8 %all-to-all-start.3 = ((bf16[2,16,24,2048]{3,2,0,1:T(8,128)(2,1)}), bf16[2,16,24,2048]{3,2,0,1:T(8,128)(2,1)}, u32[]{:S(2)}, u32[]{:S(2)}) async-start(bf16[2,16,24,2048]{3,2,0,1:T(8,128)(2,1)} %copy.52), calls=%async_computation.4 | async-start | bytes 6291456 | tf_op jit(solution)/shard_map/all_to_all | solution.py:91
  454.3 170.0 %reduce-scatter.12.cloned.1.call-start = ((), (), s32[]{:S(2)}) async-start(), calls=%async_computation.12 | async-start | bytes 786432 | tf_op jit(solution)/shard_map/reduce_scatter | solution.py:105
  499.3 125.0 %reduce-scatter.14.cloned.1.call-start = ((), (), s32[]{:S(2)}) async-start(), calls=%async_computation.13 | async-start | bytes 786432 | tf_op jit(solution)/shard_map/reduce_scatter | solution.py:108
Sparse Core Ops, SparseCore 0:
  9.6 81.4 all-gather.3
  92.6 80.3 all-gather.5
  174.5 80.3 all-gather.7
  295.9 77.1 reduce-scatter.15
  375.2 77.1 reduce-scatter.17
  454.5 77.1 reduce-scatter.19
  534.5 14.6 reduce-scatter.11
  568.8 12.8 reduce-scatter.13
where the time goes:
time: 644 us; the launch traced here: 631 us
  local copies, waits for them, and re-layouts  246 us (38%)
  waiting for transfers between devices  231 us (36%)
  matrix products  74.7 us (12%)
  other arithmetic  36.8 us (6%)
  starting transfers between devices  22.3 us (3%)
  between operations  14.6 us (2%)
    unnamed x30, local copies, waits for them, and re-layouts  146 us
    gather x2, local copies, waits for them, and re-layouts, gather_share(): buffer.at[slots, target, local_within].get(mode='fill', fill_value=0)  71.1 us
    all_to_all x1, waiting for transfers between devices, body(): lax.all_to_all(scatter_share(weighted), 'expert', split_axis=1, concat_ax...  65.4 us
    all_to_all x1, waiting for transfers between devices, body(): lax.all_to_all(out_full.astype(jnp.bfloat16).reshape(share_shape), 'exper...  56 us
    all_to_all x1, waiting for transfers between devices, body(): lax.all_to_all(scatter_share(x_rows), 'expert', split_axis=1, concat_axis...  42.8 us
    all_gather x1, waiting for transfers between devices, body(): lax.all_gather(down_weight, 'dp', axis=2, tiled=True)  39.7 us
    all_to_all x1, waiting for transfers between devices, body(): lax.all_to_all(row_full.astype(jnp.bfloat16).reshape(share_shape), 'exper...  25.2 us
    unnamed x2, other arithmetic  22.5 us
  transfers between devices with their start and end apart: 12, of which 5 were waited for; matrix products, arithmetic and copies ran while one was open for 50% of the time, Pallas kernels for 0%

commit v1 on v0

--- a/solution.py
+++ b/solution.py
@@ -2,6 +2,78 @@
 import jax.numpy as jnp
 from jax import lax
 from jax.sharding import PartitionSpec as P
+
+
+def dot(a, b, dims):
+    return lax.dot_general(a, b, (dims, ((), ())), preferred_element_type=jnp.float32)
+
+
+def body_whole(tokens, routing, route_gates, gate_weight, up_weight, down_weight, cotangent):
+    local_count = gate_weight.shape[0]
+    first = lax.axis_index("expert") * local_count
+
+    all_tokens = lax.all_gather(tokens, "expert", axis=0, tiled=True)
+    picks = routing.shape[1]
+    routes = jnp.concatenate([routing.astype(jnp.float32), route_gates], axis=1)
+    all_routes = lax.all_gather(routes, "expert", axis=0, tiled=True)
+    all_routing, all_gates = all_routes[:, :picks].astype(jnp.int32), all_routes[:, picks:]
+    all_cotangent = lax.all_gather(cotangent, "expert", axis=0, tiled=True)
+
+    named = [all_routing == first + j for j in range(local_count)]
+    gate_of = [
+        jnp.sum(jnp.where(named[j], all_gates, 0.0), axis=1, keepdims=True)
+        for j in range(local_count)
+    ]
+
+    saved = []
+    mixed_part = None
+    for j in range(local_count):
+        gate_pre = dot(all_tokens, gate_weight[j], ((1,), (0,)))
+        up_pre = dot(all_tokens, up_weight[j], ((1,), (0,)))
+        sigmoid_gate = jax.nn.sigmoid(gate_pre)
+        active = gate_pre * sigmoid_gate
+        hidden = active * up_pre
+        weighted_hidden = (gate_of[j] * hidden).astype(jnp.bfloat16)
+        saved.append((gate_pre.astype(jnp.bfloat16), up_pre.astype(jnp.bfloat16), weighted_hidden))
+    hidden_cat = jnp.concatenate([s[2] for s in saved], axis=1)
+    down_cat = jnp.concatenate([down_weight[j] for j in range(local_count)], axis=1)
+    mixed_part = dot(hidden_cat, down_cat, ((1,), (1,))).astype(jnp.bfloat16)
+    mixed_rows = lax.psum_scatter(mixed_part, "expert", scatter_dimension=0, tiled=True)
+
+    grads = []
+    gates_part = 0.0
+    for j in range(local_count):
+        gate_pre, up_pre, weighted_hidden = saved[j]
+        gate_pre, up_pre = gate_pre.astype(jnp.float32), up_pre.astype(jnp.float32)
+        raw = dot(all_cotangent, down_weight[j], ((1,), (0,)))
+        sigmoid_gate = jax.nn.sigmoid(gate_pre)
+        active = gate_pre * sigmoid_gate
+        pair = jnp.sum(raw * (active * up_pre), axis=1, keepdims=True)
+        gates_part = gates_part + jnp.where(named[j], pair, 0.0)
+        dhidden = gate_of[j] * raw
+        d_gate = (dhidden * up_pre * sigmoid_gate * (1.0 + gate_pre * (1.0 - sigmoid_gate))).astype(
+            jnp.bfloat16
+        )
+        d_up = (dhidden * active).astype(jnp.bfloat16)
+        grads.append((d_gate, d_up))
+    d_cat = jnp.concatenate([g for pair in grads for g in pair], axis=1)
+    w_cat = jnp.concatenate(
+        [w for j in range(local_count) for w in (gate_weight[j], up_weight[j])], axis=1
+    )
+    token_part = dot(d_cat, w_cat, ((1,), (1,))).astype(jnp.bfloat16)
+    token_rows = lax.psum_scatter(token_part, "expert", scatter_dimension=0, tiled=True)
+    mixed = lax.psum_scatter(mixed_rows, "dp", scatter_dimension=1, tiled=True)
+    token_grad = lax.psum_scatter(token_rows, "dp", scatter_dimension=1, tiled=True)
+    gates_grad = lax.psum(
+        lax.psum_scatter(gates_part, "expert", scatter_dimension=0, tiled=True), "dp"
+    )
+
+    grad_g = jnp.stack([dot(all_tokens, g, ((0,), (0,))).astype(jnp.bfloat16) for g, _ in grads])
+    grad_u = jnp.stack([dot(all_tokens, u, ((0,), (0,))).astype(jnp.bfloat16) for _, u in grads])
+    grad_d = jnp.stack(
+        [dot(all_cotangent, s[2], ((0,), (0,))).astype(jnp.bfloat16) for s in saved]
+    )
+    return (mixed, token_grad, gates_grad, grad_g, grad_u, grad_d)
 
 
 def expert_forward(slot_rows, w_gate, w_up, w_down):
@@ -29,7 +101,7 @@
     return (row_part, (grad_g, grad_u, grad_d))
 
 
-def body(tokens, routing, route_gates, gate_weight, up_weight, down_weight, cotangent):
+def body_slots(tokens, routing, route_gates, gate_weight, up_weight, down_weight, cotangent):
     rows_here, width = tokens.shape
     picks = routing.shape[1]
     local_count = gate_weight.shape[0]
@@ -129,6 +201,11 @@
     return (mixed, token_grad, gates_grad, grad_g, grad_u, grad_d)
 
 
+def body(tokens, *rest):
+    held = 8 * tokens.size * tokens.dtype.itemsize * lax.axis_size("expert")
+    return (body_whole if held < 1 << 27 else body_slots)(tokens, *rest)
+
+
 def solution(mesh):
     in_specs = (
         P("expert", None),

time: 644 us -> 519 us (0.81); the launches traced: 631 us -> 515 us
  local copies, waits for them, and re-layouts: 246 us -> 21 us
  waiting for transfers between devices: 231 us -> 330 us
  matrix products: 74.7 us -> 111 us
  starting transfers between devices: 22.3 us -> 0.66 us
  other arithmetic: 36.8 us -> 15.2 us
  blocking collectives: 5.73 us -> 22.7 us
    reduce_scatter x2 -> x5, waiting for transfers between devices: 0.01 us -> 224 us  [the longest x1 86.5 us: body_whole(): lax.psum_scatter(mixed_part, 'expert', scatter_dimension=0, tiled=True)]
    all_to_all x4 -> x0, waiting for transfers between devices: 189 us -> none  [the longest x1 65.4 us: body(): lax.all_to_all(scatter_share(weighted), 'expert', split_axis=1, concat_ax...]
    unnamed x30 -> x39, local copies, waits for them, and re-layouts: 146 us -> 15 us
    gather x2 -> x0, local copies, waits for them, and re-layouts: 71.1 us -> none  [gather_share(): buffer.at[slots, target, local_within].get(mode='fill', fill_value=0)]
    all_gather x3 -> x2, waiting for transfers between devices: 39.7 us -> 104 us  [the longest x1 52.4 us: body_whole(): all_tokens = lax.all_gather(tokens, 'expert', axis=0, tiled=True)]
    dot_general x11 -> x14, matrix products: 74.7 us -> 111 us  [dot(): lax.dot_general(a, b, (dims, ((), ())), preferred_element_type=jnp.float32)]
    unnamed x2 -> x1, other arithmetic: 22.5 us -> 0.01 us
    all_to_all x4 -> x0, starting transfers between devices: 21.5 us -> none  [the longest x1 6.32 us: body(): lax.all_to_all(scatter_share(x_rows), 'expert', split_axis=1, concat_axis...]
  transfers between devices with their start and end apart: 12 -> 7, of which waited for: 5 -> 7; matrix products, arithmetic and copies ran while one was open for 50% -> 18% of each run, Pallas kernels for 0% -> 0%
where the time goes in v1:
time: 519 us; the launch traced here: 515 us
  waiting for transfers between devices  330 us (64%)
  matrix products  111 us (21%)
  blocking collectives  22.7 us (4%)
  local copies, waits for them, and re-layouts  21 us (4%)
  other arithmetic  15.2 us (3%)
  between operations  14.6 us (3%)
    dot_general x14, matrix products, dot(): lax.dot_general(a, b, (dims, ((), ())), preferred_element_type=jnp.float32)  111 us
    reduce_scatter x1, waiting for transfers between devices, body_whole(): lax.psum_scatter(mixed_part, 'expert', scatter_dimension=0, tiled=True)  86.5 us
    reduce_scatter x1, waiting for transfers between devices, body_whole(): lax.psum_scatter(token_part, 'expert', scatter_dimension=0, tiled=True)  63.9 us
    all_gather x1, waiting for transfers between devices, body_whole(): all_tokens = lax.all_gather(tokens, 'expert', axis=0, tiled=True)  52.4 us
    all_gather x1, waiting for transfers between devices, body_whole(): all_cotangent = lax.all_gather(cotangent, 'expert', axis=0, tiled=True)  51.9 us
    reduce_scatter x1, waiting for transfers between devices, body_whole(): lax.psum_scatter(gates_part, 'expert', scatter_dimension=0, tiled=True)  44 us
    reduce_scatter x1, waiting for transfers between devices, body_whole(): mixed = lax.psum_scatter(mixed_rows, 'dp', scatter_dimension=1, tiled=True)  17.5 us
    all_gather x1, blocking collectives, body_whole(): all_routes = lax.all_gather(routes, 'expert', axis=0, tiled=True)  17 us
  transfers between devices with their start and end apart: 7, of which 7 were waited for; matrix products, arithmetic and copies ran while one was open for 18% of the time, Pallas kernels for 0%

profile of v1, /device:TPU:16, one launch (start us, length us, event | category | flops | bytes accessed | tf_op | source)
XLA Modules:
  0.0 514.6 jit_solution(18226163196381106546)
XLA Ops:
  7.2 0.0 all-gather.3.cloned.1.call-start
  7.2 0.7 all-gather.3.cloned.1.call-update
  7.9 0.0 all-gather.5.cloned.1.call-start
  7.9 0.7 all-gather.5.cloned.1.call-update
  8.6 0.0 reduce-scatter.10.cloned.1.call-start
  8.7 0.7 convert_element_type.90
  9.4 0.7 pad_maximum_fusion.3
  10.1 17.0 %all_gather.9 = f32[2048,16]{0,1:T(8,128)S(1)} all-gather(f32[128,16]{0,1:T(8,128)S(1)} %pad_maximum_fusion.3), channel_id=1, replica_groups=mesh['dp'=2,'expert'=16] {'expert'}, dimensions={0}, use_global_device_ids=true | all-gather | bytes 139264 | tf_op jit(solution)/shard_map/all_gather | solution.py:18
  27.1 5.7 %slice_bitcast_fusion.4 = (bf16[2048,384]{1,0:T(8,128)(2,1)}, bf16[2048,384]{1,0:T(8,128)(2,1)}, bf16[2048,384]{1,0:T(8,128)(2,1)}, bf16[2048,384]{1,0:T(8,128)(2,1)}) fusion(bf16[2,2048,384]{2,1,0:T(8,128)(2,1)} %param.11, bf16[2,2048,384]{2,1,0:T(8,128)(2,1)} %param.10), kind=kLoop, calls=%fused_computation.73 | loop fusion | bytes 12582912 | tf_op jit(solution)/shard_map/squeeze | solution.py:32
  32.9 52.4 %all-gather.3.cloned.1.call-done = bf16[2048,2048]{1,0:T(8,128)(2,1)} async-done(((bf16[128,2048]{1,0:T(8,128)(2,1)}), bf16[2048,2048]{1,0:T(8,128)(2,1)}) %all-gather.3.cloned.1.call-update) | async-done | bytes 8388624 | tf_op jit(solution)/shard_map/all_gather | solution.py:15
  85.2 6.7 %fusion.50 = f32[2048,384]{0,1:T(8,128)S(1)} fusion(bf16[2048,2048]{1,0:T(8,128)(2,1)} %all-gather.3.cloned.1.call-done, bf16[2,2048,384]{2,1,0:T(8,128)(2,1)} %param.10), kind=kOutput, calls=%fused_computation.86 | convolution fusion | flops 3221225472 | bytes 13107200 | tf_op jit(solution)/shard_map/dot_general | solution.py:8
  92.0 0.0 copy-done.5
  92.0 0.5 copy-done.15
  92.5 5.3 %fusion.51 = f32[2048,384]{0,1:T(8,128)} fusion(bf16[2048,2048]{1,0:T(8,128)(2,1)S(1)} %copy-done.15, bf16[2,2048,384]{2,1,0:T(8,128)(2,1)S(1)} %copy-done.5), kind=kOutput, calls=%fused_computation.87 | convolution fusion | flops 3221225472 | bytes 13107200 | tf_op jit(solution)/shard_map/dot_general | solution.py:8
  97.8 0.0 copy-done.4
  97.8 5.3 %fusion.48 = f32[2048,384]{0,1:T(8,128)} fusion(bf16[2048,2048]{1,0:T(8,128)(2,1)S(1)} %copy-done.15, bf16[2,2048,384]{2,1,0:T(8,128)(2,1)S(1)} %copy-done.4), kind=kOutput, calls=%fused_computation.84 | convolution fusion | flops 3221225472 | bytes 13107200 | tf_op jit(solution)/shard_map/dot_general | solution.py:8
  103.1 5.3 %fusion.49 = f32[2048,384]{0,1:T(8,128)} fusion(bf16[2048,2048]{1,0:T(8,128)(2,1)S(1)} %copy-done.15, bf16[2,2048,384]{2,1,0:T(8,128)(2,1)S(1)} %copy-done.5), kind=kOutput, calls=%fused_computation.85 | convolution fusion | flops 3221225472 | bytes 13107200 | tf_op jit(solution)/shard_map/dot_general | solution.py:8
  108.4 51.9 %all-gather.5.cloned.1.call-done = bf16[2048,2048]{1,0:T(8,128)(2,1)} async-done(((bf16[128,2048]{1,0:T(8,128)(2,1)}), bf16[2048,2048]{1,0:T(8,128)(2,1)}) %all-gather.5.cloned.1.call-update) | async-done | bytes 8388624 | tf_op jit(solution)/shard_map/all_gather | solution.py:20
  160.3 9.6 %fusion.23 = (f32[2048]{0:T(1024)S(1)}, f32[2048,384]{0,1:T(8,128)S(1)}) fusion(f32[2048,384]{0,1:T(8,128)} %fusion.51, f32[2048,384]{0,1:T(8,128)S(1)} %fusion.50, bf16[2048,2048]{1,0:T(8,128)(2,1)} %all-gather.5.cloned.1.call-done, bf16[2,2048,384]{2,1,0:T(8,128)(2,1)} %param.12), kind=kOutput, calls=%fused_computation.35 | convolution fusion | flops 3229874176 | bytes 19406848 | tf_op jit(solution)/shard_map/dot_general | solution.py:8
  169.9 0.0 copy-start
  170.0 9.9 %fusion.18 = (f32[2048]{0:T(1024)S(1)}, f32[2048,384]{0,1:T(8,128)}) fusion(f32[2048,384]{0,1:T(8,128)S(1)} %copy-done.2, f32[2048,384]{0,1:T(8,128)S(1)} %copy-done.1, bf16[2048,2048]{1,0:T(8,128)(2,1)} %all-gather.5.cloned.1.call-done, bf16[2,2048,384]{2,1,0:T(8,128)(2,1)} %param.12), kind=kOutput, calls=%fused_computation.30 | convolution fusion | flops 3229874176 | bytes 19406848 | tf_op jit(solution)/shard_map/dot_general | solution.py:8
  179.9 0.7 select_add_fusion
  180.6 8.7 %fusion.16 = (bf16[2048,384]{0,1:T(8,128)(2,1)}, bf16[2048,384]{0,1:T(8,128)(2,1)}, bf16[2048,384]{0,1:T(8,128)(2,1)}, bf16[2048,384]{0,1:T(8,128)(2,1)}, bf16[2...) fusion(f32[2048,384]{0,1:T(8,128)} %get-tuple-element.32, f32[2048]{0:T(1024)S(1)} %get-tuple-element.12, ...), kind=kLoop, calls=%fused_computation.28 | loop fusion | flops 39321600 | bytes 28327936 | tf_op jit(solution)/shard_map/convert_element_type | solution.py:54
  189.3 19.9 %convolution_convert_fusion = bf16[2048,2048]{1,0:T(8,128)(2,1)} fusion(bf16[2048,384]{0,1:T(8,128)(2,1)} %get-tuple-element.33, bf16[2048,384]{0,1:T(8,128)(2,1)} %get-tuple-element.35, bf16[2048,384]{0,1:T(8,128)(2,1)} %get-tuple-element.19, bf16[2048,384]{0,1:T(8,128)(2,1)} %get-tuple-element.17, bf16[2048,384]{1,0:T(8,128)(2,1)} %get-tuple-element.26, ...), kind=kOutput, calls=%fused_computation | convolution fusion | flops 12939427840 | bytes 20971520 | tf_op jit(solution)/shard_map/dot_general | solution.py:8
  209.2 0.0 reduce-scatter.10.cloned.1.call-update
  209.2 0.0 reduce-scatter.6.cloned.1.call-start
  209.3 1.8 copy-done.3
  211.1 0.3 slice_bitcast_fusion.1
  211.4 1.1 copy-done.8
  212.5 0.5 copy-done.10
  213.0 9.1 %convolution_convert_fusion.1 = bf16[2048,2048]{1,0:T(8,128)(2,1)} fusion(bf16[2048,384]{0,1:T(8,128)(2,1)S(1)} %copy-done.8, bf16[2048,384]{0,1:T(8,128)(2,1)S(1)} %copy-done.10, bf16[2048,384]{1,0:T(8,128)(2,1)S(1)} %get-tuple-element.28, bf16[2048,384]{1,0:T(8,128)(2,1)S(1)} %get-tuple-element.27), kind=kOutput, calls=%fused_computation.1 | convolution fusion | flops 6459228160 | bytes 14680064 | tf_op jit(solution)/shard_map/dot_general | solution.py:8
  222.1 0.0 reduce-scatter.6.cloned.1.call-update
  222.1 0.0 reduce-scatter.14.cloned.1.call-start
  222.2 0.5 reduce-scatter.14.cloned.1.call-update
  222.7 0.0 copy-start.12
  222.7 0.2 reduce-scatter.12.cloned.1.call-start
  222.9 0.7 copy-done.13
  223.7 7.7 %fusion.40 = bf16[1,2048,384]{1,2,0:T(8,128)(2,1)S(1)} fusion(bf16[2048,384]{0,1:T(8,128)(2,1)S(1)} %copy-done.13, bf16[2048,2048]{1,0:T(8,128)(2,1)} %all-gather.3.cloned.1.call-done), kind=kOutput, calls=%fused_computation.65 | convolution fusion | flops 3222011904 | bytes 11534336 | tf_op jit(solution)/shard_map/dot_general | solution.py:8
  231.4 0.0 copy-start.11
  231.4 0.0 slice-start.1
  231.4 7.0 %fusion.41 = bf16[1,2048,384]{1,2,0:T(8,128)(2,1)S(1)} fusion(bf16[2048,384]{0,1:T(8,128)(2,1)S(1)} %copy-done.12, bf16[2048,2048]{1,0:T(8,128)(2,1)} %all-gather.3.cloned.1.call-done), kind=kOutput, calls=%fused_computation.66 | convolution fusion | flops 3222011904 | bytes 11534336 | tf_op jit(solution)/shard_map/dot_general | solution.py:8
  238.5 4.5 fusion.42
  242.9 4.5 fusion.43
  247.4 0.3 pad_maximum_fusion.1
  247.7 63.9 %reduce-scatter.10.cloned.1.call-done = bf16[128,2048]{1,0:T(8,128)(2,1)} async-done(((bf16[2048,2048]{1,0:T(8,128)(2,1)}), bf16[128,2048]{1,0:T(8,128)(2,1)}) %reduce-scatter.10.cloned.1.call-update) | async-done | bytes 524304 | tf_op jit(solution)/shard_map/reduce_scatter | solution.py:64
  311.6 0.0 reduce-scatter.12.cloned.1.call-update
  311.7 0.3 reduce-scatter.8.cloned.1.call-start
  311.9 3.8 pad_maximum_fusion.2
  315.8 2.8 copy.14
  318.5 4.8 copy.15
  323.3 0.0 copy-done.7
  323.3 8.8 %fusion.38 = bf16[1,2048,384]{1,2,0:T(8,128)(2,1)} fusion(bf16[2048,384]{0,1:T(8,128)(2,1)S(1)} %copy-done.7, bf16[2048,2048]{1,0:T(8,128)(2,1)} %all-gather.3.cloned.1.call-done), kind=kOutput, calls=%fused_computation.63 | convolution fusion | flops 3222011904 | bytes 11534336 | tf_op jit(solution)/shard_map/dot_general | solution.py:8
  332.1 86.5 %reduce-scatter.6.cloned.1.call-done = bf16[128,2048]{1,0:T(8,128)(2,1)} async-done(((bf16[2048,2048]{1,0:T(8,128)(2,1)}), bf16[128,2048]{1,0:T(8,128)(2,1)}) %reduce-scatter.6.cloned.1.call-update) | async-done | bytes 524304 | tf_op jit(solution)/shard_map/reduce_scatter | solution.py:41
  418.7 0.0 reduce-scatter.8.cloned.1.call-update
  418.7 0.0 copy-done.6
  418.7 0.0 copy-start.14
  418.7 6.9 %fusion.39 = bf16[1,2048,384]{1,2,0:T(8,128)(2,1)S(1)} fusion(bf16[2048,384]{0,1:T(8,128)(2,1)S(1)} %copy-done.6, bf16[2048,2048]{1,0:T(8,128)(2,1)} %all-gather.3.cloned.1.call-done), kind=kOutput, calls=%fused_computation.64 | convolution fusion | flops 3222011904 | bytes 11534336 | tf_op jit(solution)/shard_map/dot_general | solution.py:8
  425.6 0.0 copy-done.14
  425.6 0.3 pad_maximum_fusion
  425.9 2.8 copy.13
  428.7 44.0 %reduce-scatter.14.cloned.1.call-done = f32[128,8]{0,1:T(8,128)} async-done(((f32[2048,8]{0,1:T(8,128)}), f32[128,8]{0,1:T(8,128)}) %reduce-scatter.14.cloned.1.call-update) | async-done | bytes 4112 | tf_op jit(solution)/shard_map/reduce_scatter | solution.py:68
  472.7 5.6 %psum.7 = f32[128,8]{0,1:T(8,128)} all-reduce(f32[128,8]{0,1:T(8,128)} %reduce-scatter.14.cloned.1.call-done), channel_id=1, replica_groups=mesh['dp'=2,'expert'=16] {'dp'}, use_global_device_ids=true, to_apply=%region_9.10 | all-reduce | flops 1024 | bytes 8192 | tf_op jit(solution)/shard_map/psum | solution.py:67
  478.3 11.7 %reduce-scatter.12.cloned.1.call-done = bf16[128,1024]{1,0:T(8,128)(2,1)} async-done(((bf16[128,2048]{1,0:T(8,128)(2,1)}), bf16[128,1024]{1,0:T(8,128)(2,1)}) %reduce-scatter.12.cloned.1.call-update) | async-done | bytes 262160 | tf_op jit(solution)/shard_map/reduce_scatter | solution.py:66
  490.0 17.5 %reduce-scatter.8.cloned.1.call-done = bf16[128,1024]{1,0:T(8,128)(2,1)} async-done(((bf16[128,2048]{1,0:T(8,128)(2,1)}), bf16[128,1024]{1,0:T(8,128)(2,1)}) %reduce-scatter.8.cloned.1.call-update) | async-done | bytes 262160 | tf_op jit(solution)/shard_map/reduce_scatter | solution.py:65
  (23 shorter events, 0.1 us)
Async XLA Ops:
  7.2 78.1 %all-gather.3.cloned.1.call-start = ((), (), s32[]{:S(2)}) async-start(), calls=%async_computation.5 | async-start | bytes 8912896 | tf_op jit(solution)/shard_map/all_gather | solution.py:15
  7.9 152.4 %all-gather.5.cloned.1.call-start = ((), (), s32[]{:S(2)}) async-start(), calls=%async_computation.8 | async-start | bytes 8912896 | tf_op jit(solution)/shard_map/all_gather | solution.py:20
  8.6 303.0 %reduce-scatter.10.cloned.1.call-start = ((), (), s32[]{:S(2)}) async-start(), calls=%async_computation.9 | async-start | bytes 8912896 | tf_op jit(solution)/shard_map/reduce_scatter | solution.py:64
  85.2 6.7 %copy-start.5 = (bf16[2,2048,384]{2,1,0:T(8,128)(2,1)S(1)}, bf16[2,2048,384]{2,1,0:T(8,128)(2,1)}, u32[]{:S(2)}) copy-start(bf16[2,2048,384]{2,1,0:T(8,128)(2,1)} %param.11) | copy-start | bytes 9437188
  85.2 7.3 %copy-start.15 = (bf16[2048,2048]{1,0:T(8,128)(2,1)S(1)}, bf16[2048,2048]{1,0:T(8,128)(2,1)}, u32[]{:S(2)}) copy-start(bf16[2048,2048]{1,0:T(8,128)(2,1)} %all-gather.3.cloned.1.call-done) | copy-start | bytes 25165828
  92.5 5.3 %copy-start.4 = (bf16[2,2048,384]{2,1,0:T(8,128)(2,1)S(1)}, bf16[2,2048,384]{2,1,0:T(8,128)(2,1)}, u32[]{:S(2)}) copy-start(bf16[2,2048,384]{2,1,0:T(8,128)(2,1)} %param.10) | copy-start | bytes 9437188
  160.3 9.6 %copy-start.1 = (f32[2048,384]{0,1:T(8,128)S(1)}, f32[2048,384]{0,1:T(8,128)}, u32[]{:S(2)}) copy-start(f32[2048,384]{0,1:T(8,128)} %fusion.48) | copy-start | bytes 9437188
  160.3 9.6 %copy-start.2 = (f32[2048,384]{0,1:T(8,128)S(1)}, f32[2048,384]{0,1:T(8,128)}, u32[]{:S(2)}) copy-start(f32[2048,384]{0,1:T(8,128)} %fusion.49) | copy-start | bytes 9437188
  169.9 10.6 %copy-start = (f32[2048,384]{0,1:T(8,128)S(1)}, f32[2048,384]{0,1:T(8,128)}, u32[]{:S(2)}) copy-start(f32[2048,384]{0,1:T(8,128)} %fusion.51) | copy-start | bytes 9437188
  209.2 1.9 copy-start.3
  209.2 209.4 %reduce-scatter.6.cloned.1.call-start = ((), (), s32[]{:S(2)}) async-start(), calls=%async_computation.6 | async-start | bytes 8912896 | tf_op jit(solution)/shard_map/reduce_scatter | solution.py:41
  211.1 1.4 copy-start.8
  211.1 1.9 copy-start.10
  222.1 1.6 copy-start.13
  222.1 250.6 %reduce-scatter.14.cloned.1.call-start = ((), (), s32[]{:S(2)}) async-start(), calls=%async_computation.11 | async-start | bytes 69632 | tf_op jit(solution)/shard_map/reduce_scatter | solution.py:68
  222.7 8.7 %copy-start.12 = (bf16[2048,384]{0,1:T(8,128)(2,1)S(1)}, bf16[2048,384]{0,1:T(8,128)(2,1)}, u32[]{:S(2)}) copy-start(bf16[2048,384]{0,1:T(8,128)(2,1)} %get-tuple-element.33) | copy-start | bytes 4718596
  222.7 267.3 %reduce-scatter.12.cloned.1.call-start = ((), (), s32[]{:S(2)}) async-start(), calls=%async_computation.10 | async-start | bytes 786432 | tf_op jit(solution)/shard_map/reduce_scatter | solution.py:66
  223.7 14.8 %slice-start = ((s8[8388608]{0:T(1024)(128)(4,1)}), s8[4194304]{0:T(1024)(128)(4,1)S(1)}, s32[]{:S(2)}) async-start(s8[8388608]{0:T(1024)(128)(4,1)} %bitcast.64), calls=%async_computation.12 | async-start | bytes 8388608
  231.4 7.0 %copy-start.11 = (bf16[2048,384]{0,1:T(8,128)(2,1)S(1)}, bf16[2048,384]{0,1:T(8,128)(2,1)}, u32[]{:S(2)}) copy-start(bf16[2048,384]{0,1:T(8,128)(2,1)} %get-tuple-element.18) | copy-start | bytes 4718596
  231.4 7.0 %slice-start.1 = ((s8[8388608]{0:T(1024)(128)(4,1)}), s8[4194304]{0:T(1024)(128)(4,1)S(1)}, s32[]{:S(2)}) async-start(s8[8388608]{0:T(1024)(128)(4,1)} %bitcast.64), calls=%async_computation.13 | async-start | bytes 8388608
  238.4 4.5 copy-start.9
  311.7 195.8 %reduce-scatter.8.cloned.1.call-start = ((), (), s32[]{:S(2)}) async-start(), calls=%async_computation.7 | async-start | bytes 786432 | tf_op jit(solution)/shard_map/reduce_scatter | solution.py:65
  318.5 4.8 copy-start.7
  323.3 95.4 %copy-start.6 = (bf16[2048,384]{0,1:T(8,128)(2,1)S(1)}, bf16[2048,384]{0,1:T(8,128)(2,1)}, u32[]{:S(2)}) copy-start(bf16[2048,384]{0,1:T(8,128)(2,1)} %get-tuple-element.35) | copy-start | bytes 4718596
  418.7 6.9 %copy-start.14 = (bf16[1,2048,384]{1,2,0:T(8,128)(2,1)S(1)}, bf16[1,2048,384]{1,2,0:T(8,128)(2,1)}, u32[]{:S(2)}) copy-start(bf16[1,2048,384]{1,2,0:T(8,128)(2,1)} %fusion.38) | copy-start | bytes 4718596
Sparse Core Ops, SparseCore 0:
  10.1 75.0 all-gather.2
  87.4 72.8 all-gather.4
  209.4 102.2 reduce-scatter.9
  315.6 103.0 reduce-scatter.5
  421.9 50.8 reduce-scatter.13
  475.4 14.6 reduce-scatter.11
  492.8 14.6 reduce-scatter.7
